TPU v7x, 32 devices: a whole 2x2x4 slice. The times are simulated.
32 devices in a mesh: tile: 8 (over z, y), depth: 4 (over x, core).
Axes of the slice: x: 2, y: 2, z: 4, core: 2. Of those that a mesh axis runs over, the one named last changes fastest.
Arguments:
- positions: float32 [3, 16384], P(None, 'tile'), may hold values from -4 to 4
- log_scales: float32 [3, 16384], P(None, 'tile'), may hold values from -2 to 0
- opacity_logits: float32 [1, 16384], P(None, 'tile'), may hold values from -3 to 1.5
- colors: float32 [3, 16384], P(None, 'tile'), may hold values from 0 to 1
- first_moment: float32 [10, 16384], P(None, 'tile'), may hold values from -3 to 3
- second_moment: float32 [10, 16384], P(None, 'tile'), may hold values from 0.01 to 1
- cameras: float32 [4, 2, 4], replicated, may hold values from -6.4 to 6.4
- background: float32 [3], replicated, may hold values from 0 to 1
- target: float32 [32, 3, 1024], P('tile'), may hold values from 0 to 1
- tile_view: int32 [32], P('tile'), may hold values from 0 to 3
- tile_length: int32 [32], P('tile'), may hold values from 128 to 512
- list_owner: int32 [4, 32, 128, 1], P('depth', 'tile'), may hold values from 0 to 7; in each aligned block of 512 rows (0 to 511, 512 to 1023, ..., all dimensions but the last counted through in order) at most 160 rows name the same one
- list_row: int32 [4, 32, 128], P('depth', 'tile'), may hold values from 0 to 2047
Outputs:
- image: float32 [32, 3, 1024], P('tile')
- new_params: float32 [10, 16384], P(None, 'tile')
- new_first: float32 [10, 16384], P(None, 'tile')
- new_second: float32 [10, 16384], P(None, 'tile')
Inputs may be any that keep to these rules, and one draw needn't show every extreme that they name: `list_owner`: within the entries of one device's block (one depth slab of the tiles of one tile index), no owner is named more than 160 times, a bound that some block reaches.
All inputs are finite; a program needn't handle non-finite values.
Results may differ from a plain program's by a relative error of at most 0.00008.
Values sent between devices are 32-bit elements; how exact they have to be, the bound alone decides.
A program may use at most 64 MiB of HBM per device.

v0:
```python
import jax
import jax.numpy as jnp
from jax import lax
from jax.sharding import PartitionSpec as P

TILE_SIDE = 32


def project(params, cams):
    position = params[0:3]
    variance = jnp.exp(2.0 * params[3:6])
    first_row = cams[:, 0, 0:3].T
    second_row = cams[:, 1, 0:3].T
    center_x = jnp.sum(first_row * position, axis=0) + cams[:, 0, 3] + 0.5 * TILE_SIDE
    center_y = jnp.sum(second_row * position, axis=0) + cams[:, 1, 3] + 0.5 * TILE_SIDE
    cov_xx = jnp.sum(first_row * first_row * variance, axis=0) + 0.3
    cov_xy = jnp.sum(first_row * second_row * variance, axis=0)
    cov_yy = jnp.sum(second_row * second_row * variance, axis=0) + 0.3
    determinant = cov_xx * cov_yy - cov_xy * cov_xy
    return jnp.stack(
        [
            center_x,
            center_y,
            cov_yy / determinant,
            -cov_xy / determinant,
            cov_xx / determinant,
            jax.nn.sigmoid(params[6]),
            params[7],
            params[8],
            params[9],
        ]
    )


def coverage(screen, alive, pixels):
    pixel = jnp.arange(pixels, dtype=jnp.int32)
    pixel_x = (pixel % TILE_SIDE).astype(jnp.float32) + 0.5
    pixel_y = (pixel // TILE_SIDE).astype(jnp.float32) + 0.5
    offset_x = pixel_x[:, None] - screen[0][None, :]
    offset_y = pixel_y[:, None] - screen[1][None, :]
    quadric = (
        screen[2][None, :] * offset_x * offset_x
        + 2.0 * screen[3][None, :] * offset_x * offset_y
        + screen[4][None, :] * offset_y * offset_y
    )
    falloff = jnp.exp(-0.5 * quadric)
    alpha = screen[5][None, :] * falloff * alive[None, :]
    return (offset_x, offset_y, falloff, alpha)


def running_sum(values, triangle):
    rows = values.shape[0]
    width = triangle.shape[0]
    blocks = values.reshape(rows, values.shape[1] // width, width)
    inner = jnp.einsum("pbk,kj->pbj", blocks, triangle, precision=lax.Precision.HIGHEST)
    sums = jnp.sum(blocks, axis=2)
    lead = jnp.cumsum(sums, axis=1) - sums
    return (inner + lead[:, :, None]).reshape(rows, values.shape[1])


def adam_update(param, first, second, gradient):
    new_first = 0.9 * first + 0.1 * gradient
    new_second = 0.999 * second + 0.001 * gradient * gradient
    corrected = new_first / (1.0 - 0.9**10) / (jnp.sqrt(new_second / (1.0 - 0.999**10)) + 1e-08)
    return (param - 0.05 * corrected, new_first, new_second)


def body(
    positions,
    log_scales,
    opacity_logits,
    colors,
    first_moment,
    second_moment,
    cameras,
    background,
    target,
    tile_view,
    tile_length,
    list_owner,
    list_row,
):
    tiles_here = target.shape[0]
    pixels = target.shape[2]
    slab = list_row.shape[2]
    owner_count = lax.axis_size("tile")
    depth_count = lax.axis_size("depth")
    depth_index = lax.axis_index("depth")
    capacity = max(2, 5 * tiles_here * slab // (2 * owner_count))
    highest = lax.Precision.HIGHEST
    params = jnp.concatenate([positions, log_scales, opacity_logits, colors], axis=0)
    owner = list_owner.reshape(-1)
    wanted = list_row.reshape(-1)
    viewed = jnp.repeat(tile_view, slab)
    onehot = (owner[:, None] == jnp.arange(owner_count, dtype=jnp.int32)[None, :]).astype(jnp.int32)
    rank = jnp.sum((jnp.cumsum(onehot, axis=0) - onehot) * onehot, axis=1)
    slot = owner * capacity + rank
    request = (
        jnp.zeros((2, owner_count * capacity), jnp.int32)
        .at[:, slot]
        .set(jnp.stack([wanted, viewed]))
    )
    request = request.reshape(2, owner_count, capacity)
    received = lax.all_to_all(request, "tile", split_axis=1, concat_axis=1, tiled=True)
    rows_in = received[0].reshape(-1)
    views_in = received[1].reshape(-1)
    screen = project(params[:, rows_in], cameras[views_in])
    screen = screen.reshape(9, received.shape[1], received.shape[2])
    fetched = lax.all_to_all(screen, "tile", split_axis=1, concat_axis=1, tiled=True)
    entry = fetched.reshape(9, -1)[:, slot].reshape(9, tiles_here, slab).transpose(1, 0, 2)
    order = jnp.arange(slab, dtype=jnp.int32)
    strict = (order[:, None] < order[None, :]).astype(jnp.float32)
    inclusive = (order[:, None] <= order[None, :]).astype(jnp.float32)

    def forward(args):
        screen, alive = args
        offset_x, offset_y, falloff, alpha = coverage(screen, alive, pixels)
        leak = jnp.log1p(-alpha)
        before = running_sum(leak, strict)
        weight = alpha * jnp.exp(before)
        color = jnp.einsum("ck,pk->cp", screen[6:9], weight, precision=highest)
        return (jnp.sum(leak, axis=1), color)

    def backward(args):
        screen, alive, start_log, start_color, whole, miss = args
        offset_x, offset_y, falloff, alpha = coverage(screen, alive, pixels)
        leak = jnp.log1p(-alpha)
        local = running_sum(leak, strict)
        carried = jnp.exp(start_log)[:, None]
        inside = jnp.exp(local)
        trans = carried * inside
        weight = alpha * trans
        local_weight = alpha * inside
        d_alpha = jnp.zeros_like(alpha)
        for channel in range(3):
            shade = screen[6 + channel][None, :]
            upto = running_sum(local_weight * shade, inclusive)
            behind = whole[channel][:, None] - start_color[channel][:, None] - carried * upto
            d_alpha = d_alpha + miss[channel][:, None] * (trans * shade - behind / (1.0 - alpha))
        d_color = jnp.einsum("cp,pk->ck", miss, weight, precision=highest)
        d_quad = d_alpha * (-0.5 * alpha)
        d_opacity = jnp.sum(d_alpha * falloff * alive[None, :], axis=0)
        d_center_x = jnp.sum(
            d_quad * -2.0 * (screen[2][None, :] * offset_x + screen[3][None, :] * offset_y), axis=0
        )
        d_center_y = jnp.sum(
            d_quad * -2.0 * (screen[3][None, :] * offset_x + screen[4][None, :] * offset_y), axis=0
        )
        d_conic_a = jnp.sum(d_quad * offset_x * offset_x, axis=0)
        d_conic_b = jnp.sum(d_quad * 2.0 * offset_x * offset_y, axis=0)
        d_conic_c = jnp.sum(d_quad * offset_y * offset_y, axis=0)
        return jnp.concatenate(
            [
                jnp.stack([d_center_x, d_center_y, d_conic_a, d_conic_b, d_conic_c, d_opacity]),
                d_color,
            ],
            axis=0,
        )

    quarter = tiles_here // depth_count
    whole_entry = lax.all_to_all(entry, "depth", split_axis=0, concat_axis=2, tiled=True)
    first_tile = depth_index * quarter
    own_length = lax.dynamic_slice_in_dim(tile_length, first_tile, quarter, 0)
    full_place = jnp.arange(slab * depth_count, dtype=jnp.int32)
    own_live = (full_place[None, :] < own_length[:, None]).astype(jnp.float32)
    own_log, own_color = lax.map(forward, (whole_entry, own_live))
    own_image = own_color + jnp.exp(own_log)[:, None, :] * background[None, :, None]
    own_error = own_image - lax.dynamic_slice_in_dim(target, first_tile, quarter, 0)
    zero_log = jnp.zeros_like(own_log)
    zero_color = jnp.zeros_like(own_color)
    own_grad = lax.map(
        backward, (whole_entry, own_live, zero_log, zero_color, own_image, own_error)
    )
    entry_grad = lax.all_to_all(own_grad, "depth", split_axis=2, concat_axis=0, tiled=True)
    image = lax.all_gather(own_image, "depth", axis=0, tiled=True)
    flat_grad = entry_grad.transpose(1, 0, 2).reshape(9, -1)
    outgoing = jnp.zeros((9, owner_count * capacity), jnp.float32).at[:, slot].set(flat_grad)
    outgoing = outgoing.reshape(9, owner_count, capacity)
    incoming = lax.all_to_all(outgoing, "tile", split_axis=1, concat_axis=1, tiled=True)
    rows_in = received[0].reshape(-1)
    views_in = received[1].reshape(-1)
    chosen_cams = cameras[views_in]
    unused, pullback = jax.vjp(lambda chosen: project(chosen, chosen_cams), params[:, rows_in])
    (slot_grad,) = pullback(incoming.reshape(9, -1))
    gradient = jnp.zeros_like(params).at[:, rows_in].add(slot_grad)
    gradient = lax.psum(gradient, "depth")
    new_params, new_first, new_second = adam_update(params, first_moment, second_moment, gradient)
    return (image, new_params, new_first, new_second)


def solution(mesh):
    placed = (
        P(None, "tile"),
        P(None, "tile"),
        P(None, "tile"),
        P(None, "tile"),
        P(None, "tile"),
        P(None, "tile"),
        P(),
        P(),
        P("tile", None, None),
        P("tile"),
        P("tile"),
        P("depth", "tile", None, None),
        P("depth", "tile", None),
    )
    return jax.shard_map(
        body,
        mesh=mesh,
        in_specs=placed,
        out_specs=(P("tile", None, None), P(None, "tile"), P(None, "tile"), P(None, "tile")),
        check_vma=False,
    )
```

profile of v0, /device:TPU:0, one launch (start us, length us, event | category | flops | bytes accessed | tf_op | source)
XLA Modules:
  0.0 199.4 jit_solution(7363935695881023951)
XLA Ops:
  7.9 1.1 reduce-window.6
  12.3 1.9 scatter_custom_fusion
  15.2 7.3 %all-to-all-start = ((s32[2,8,160]{2,0,1:T(2,128)}), s32[2,8,160]{2,0,1:T(2,128)S(1)}, u32[]{:S(2)}, u32[]{:S(2)}) async-start(s32[2,8,160]{2,0,1:T(2,128)} %copy.152), calls=%async_computation | async-start | bytes 32768 | tf_op jit(solution)/shard_map/all_to_all | solution.py:104
  24.3 4.7 %all-to-all-done = s32[2,8,160]{2,0,1:T(2,128)S(1)} async-done(((s32[2,8,160]{2,0,1:T(2,128)}), s32[2,8,160]{2,0,1:T(2,128)S(1)}, u32[]{:S(2)}, u32[]{:S(2)}) %all-to-all-start) | async-done | bytes 10272 | tf_op jit(solution)/shard_map/all_to_all | solution.py:104
  29.2 4.3 %gather_fusion = f32[1280,2,4]{2,1,0:T(2,128)S(1)} fusion(f32[4,2,4]{2,1,0:T(2,128)S(1)} %copy-done.1, s32[2048]{0:T(1024)S(1)} %pad_clamp_fusion.1), kind=kCustom, calls=%fused_computation | custom fusion | bytes 87040 | tf_op jit(solution)/shard_map/gather | solution.py:107
  33.6 1.8 fusion.84
  35.3 36.3 %slice_reduce_fusion = (f32[1280]{0:T(1024)S(1)}, f32[1280]{0:T(1024)S(1)}) fusion(f32[1280,2,4]{2,1,0:T(2,128)S(1)} %gather_fusion), kind=kLoop, calls=%fused_computation.71 | loop fusion | bytes 20480 | tf_op jit(solution)/shard_map/slice | solution.py:15
  71.6 1.3 copy.189
  73.4 2.4 %gather_fusion.1 = f32[1280,10]{1,0:T(8,128)S(1)} fusion(f32[10,2048]{0,1:T(8,128)S(1)} %copy.154, s32[2048]{0:T(1024)S(1)} %pad_clamp_fusion), kind=kCustom, calls=%fused_computation.1 | custom fusion | bytes 107520 | tf_op jit(solution)/shard_map/gather | solution.py:107
  78.0 3.5 %all-to-all-start.1 = ((f32[8,1,1440]{2,1,0:T(1,128)}), f32[8,1,1440]{2,1,0:T(1,128)S(1)}, u32[]{:S(2)}, u32[]{:S(2)}) async-start(f32[8,1,1440]{2,1,0:T(1,128)} %reshape.1452), calls=%async_computation.1 | async-start | bytes 98304 | tf_op jit(solution)/shard_map/all_to_all | solution.py:109
  82.2 5.9 %all-to-all-done.1 = f32[8,1,1440]{2,1,0:T(1,128)S(1)} async-done(((f32[8,1,1440]{2,1,0:T(1,128)}), f32[8,1,1440]{2,1,0:T(1,128)S(1)}, u32[]{:S(2)}, u32[]{:S(2)}) %all-to-all-start.1) | async-done | bytes 46112 | tf_op jit(solution)/shard_map/all_to_all | solution.py:109
  89.7 1.0 gather_fusion.2
  91.5 3.3 %all-to-all-start.2 = ((f32[4,9,128]{2,1,0:T(8,128)}), f32[4,9,128]{2,1,0:T(8,128)S(1)}, u32[]{:S(2)}, u32[]{:S(2)}) async-start(f32[4,9,128]{2,1,0:T(8,128)} %bitcast.21), calls=%async_computation.2 | async-start | bytes 65536 | tf_op jit(solution)/shard_map/all_to_all | solution.py:161
  95.5 3.2 %all-to-all-done.2 = f32[4,9,128]{2,1,0:T(8,128)S(1)} async-done(((f32[4,9,128]{2,1,0:T(8,128)}), f32[4,9,128]{2,1,0:T(8,128)S(1)}, u32[]{:S(2)}, u32[]{:S(2)}) %all-to-all-start.2) | async-done | bytes 18464 | tf_op jit(solution)/shard_map/all_to_all | solution.py:161
  98.7 2.0 fusion.28
  100.8 5.9 %multiply_reduce_fusion.3 = (f32[1024,4]{0,1:T(4,128)S(1)}, f32[1024,4]{0,1:T(4,128)S(1)}, f32[1024,4]{0,1:T(4,128)S(1)}, f32[1024,4,128]{0,2,1:T(8,128)S(1)}, f32[1024,4,128]{0,2,1:T(8,128)}) fusion(f32[4,128]{1,0:T(4,128)S(1)} %bitcast.208, f32[4,128]{1,0:T(4,128)S(1)} %bitcast.188, f32[4,128]{1,0:T(4,128)S(1)} %bitcast.185, f32[1024,4]{0,1:T(4,128)S(1)} %sub.316, ...), kind=kOutput, calls=%fused_computation.60 | convolution fusion | flops 823660544 | bytes 4288512 | tf_op jit(solution)/shard_map/while/body/eval_jaxpr/pbk,kj->pbj/dot_general | solution.py:55
  106.7 2.9 %fusion.24 = f32[1024,4,128]{0,2,1:T(8,128)} fusion(f32[1024,4,128]{0,2,1:T(8,128)S(1)} %get-tuple-element.96, f32[4,128]{1,0:T(4,128)S(1)} %bitcast.189), kind=kOutput, calls=%fused_computation.58 | convolution fusion | flops 805847040 | bytes 4196352 | tf_op jit(solution)/shard_map/while/body/eval_jaxpr/pbk,kj->pbj/dot_general | solution.py:55
  109.6 2.9 %fusion.22 = f32[1024,4,128]{0,2,1:T(8,128)} fusion(f32[1024,4,128]{0,2,1:T(8,128)S(1)} %get-tuple-element.96, f32[4,128]{1,0:T(4,128)S(1)} %bitcast.186), kind=kOutput, calls=%fused_computation.55 | convolution fusion | flops 805847040 | bytes 4196352 | tf_op jit(solution)/shard_map/while/body/eval_jaxpr/pbk,kj->pbj/dot_general | solution.py:55
  112.5 1.9 fusion.14
  114.4 1.1 copy_subtract_fusion
  115.5 1.8 fusion.56
  117.5 6.2 %multiply_multiply_fusion = (f32[1024,4,128]{0,2,1:T(8,128)S(1)}, f32[1024,4,128]{0,2,1:T(8,128)S(1)}) fusion(f32[4,128]{1,0:T(4,128)S(1)} %fusion.74, f32[4,128]{1,0:T(4,128)S(1)} %bitcast.168, f32[4,128]{1,0:T(4,128)S(1)} %bitcast.173, f32[1024]{0:T(1024)S(1)} %get-tuple-element.136, f32[4,128]{1,0:T(4,128)S(1)} %broadcast_multiply_fusion.1, ...), kind=kOutput, calls=%fused_computation.49 | convolution fusion | flops 825245696 | bytes 12701696 | tf_op jit(solution)/shard_map/while/body/eval_jaxpr/pbk,kj->pbj/dot_general | solution.py:55
  123.7 3.8 %fusion.3 = (f32[4,128]{1,0:T(4,128)S(1)}, f32[4,128]{1,0:T(4,128)S(1)}, f32[4,128]{1,0:T(4,128)S(1)}, f32[4,128]{1,0:T(4,128)S(1)}, f32[4,128]{1,0:T(4,128)S(1)}, /*index=5*/f32[4,128]{1,0:T(4,128)S(1)}) fusion(f32[1024,4,128]{0,2,1:T(8,128)S(1)} %get-tuple-element.131, f32[4,128]{1,0:T(4,128)S(1)} %bitcast.162, f32[4,128]{1,0:T(4,128)S(1)} %bitcast.169, ...), kind=kLoop, calls=%fused_computation.29 | loop fusion | flops 17298432 | bytes 4229120 | tf_op jit(solution)/shard_map/while/body/eval_jaxpr/reduce_sum | solution.py:146
  127.9 1.3 reduce.41
  129.4 6.2 %all_to_all.48 = f32[4,1,1152]{2,1,0:T(1,128)S(1)} all-to-all(f32[4,1,1152]{2,1,0:T(1,128)S(1)} %reshape.1454), channel_id=1, replica_groups=mesh['tile'=8,'depth'=4] {'depth'}, dimensions={0} | all-to-all | bytes 36864 | tf_op jit(solution)/shard_map/all_to_all | solution.py:174
  137.0 1.9 scatter_custom_fusion.1
  139.3 9.2 %all_to_all.49 = f32[8,1,1440]{2,1,0:T(1,128)S(1)} all-to-all(f32[8,1,1440]{2,1,0:T(1,128)S(1)} %reshape.1456), channel_id=1, replica_groups=mesh['tile'=8,'depth'=4] {'tile'}, dimensions={0} | all-to-all | bytes 92160 | tf_op jit(solution)/shard_map/all_to_all | solution.py:179
  150.8 9.2 %scatter_custom_fusion.2 = f32[10,2048]{0,1:T(8,128)S(1)} fusion(s32[1280]{0:T(1024)S(1)} %fusion.60, f32[1280,10]{1,0:T(8,128)S(1)} %copy.178, f32[]{:T(128)} %constant.132.clone.1), kind=kCustom, calls=%fused_computation.73 | custom fusion | flops 12800 | bytes 81924 | tf_op jit(solution)/shard_map/scatter-add | solution.py:185
  160.0 1.0 copy.179
  161.0 5.2 %all-gather.1 = f32[4,3,1024]{2,1,0:T(4,128)S(1)} all-gather(f32[1,3,1024]{2,1,0:T(4,128)S(1)} %get-tuple-element.130), channel_id=2, replica_groups=mesh['tile'=8,'depth'=4] {'depth'}, dimensions={0}, use_global_device_ids=true | all-gather | bytes 61440 | tf_op jit(solution)/shard_map/all_gather | solution.py:175
  166.8 23.9 %all-reduce.8.cloned.1.call-done = f32[10,2048]{1,0:T(8,128)} async-done(((f32[10,2048]{1,0:T(8,128)}), f32[10,2048]{1,0:T(8,128)}) %all-reduce.8.cloned.1.call-update) | async-done | bytes 81936 | tf_op jit(solution)/shard_map/psum | solution.py:186
  190.8 1.7 multiply_subtract_fusion
  (119 shorter events, 18.8 us)
Async XLA Ops:
  7.2 15.3 %copy-start = (f32[4,3,1024]{2,0,1:T(4,128)S(1)}, f32[4,3,1024]{2,0,1:T(4,128)}, u32[]{:S(2)}) copy-start(f32[4,3,1024]{2,0,1:T(4,128)} %param.21) | copy-start | bytes 147460
  7.2 16.6 %copy-start.9 = (s32[4]{0:T(128)S(1)}, s32[4]{0:T(128)}, u32[]{:S(2)}) copy-start(s32[4]{0:T(128)} %param.23) | copy-start | bytes 52
  7.2 22.0 %copy-start.1 = (f32[4,2,4]{2,1,0:T(2,128)S(1)}, f32[4,2,4]{2,1,0:T(2,128)}, u32[]{:S(2)}) copy-start(f32[4,2,4]{2,1,0:T(2,128)} %param.19) | copy-start | bytes 388
  15.2 13.9 %all-to-all-start = ((s32[2,8,160]{2,0,1:T(2,128)}), s32[2,8,160]{2,0,1:T(2,128)S(1)}, u32[]{:S(2)}, u32[]{:S(2)}) async-start(s32[2,8,160]{2,0,1:T(2,128)} %copy.152), calls=%async_computation | async-start | bytes 32768 | tf_op jit(solution)/shard_map/all_to_all | solution.py:104
  78.0 10.1 %all-to-all-start.1 = ((f32[8,1,1440]{2,1,0:T(1,128)}), f32[8,1,1440]{2,1,0:T(1,128)S(1)}, u32[]{:S(2)}, u32[]{:S(2)}) async-start(f32[8,1,1440]{2,1,0:T(1,128)} %reshape.1452), calls=%async_computation.1 | async-start | bytes 98304 | tf_op jit(solution)/shard_map/all_to_all | solution.py:109
  91.5 7.2 %all-to-all-start.2 = ((f32[4,9,128]{2,1,0:T(8,128)}), f32[4,9,128]{2,1,0:T(8,128)S(1)}, u32[]{:S(2)}, u32[]{:S(2)}) async-start(f32[4,9,128]{2,1,0:T(8,128)} %bitcast.21), calls=%async_computation.2 | async-start | bytes 65536 | tf_op jit(solution)/shard_map/all_to_all | solution.py:161
  94.8 96.0 %all-reduce.8.cloned.1.call-start = ((), (), s32[]{:S(2)}) async-start(), calls=%async_computation.5 | async-start | bytes 262144 | tf_op jit(solution)/shard_map/psum | solution.py:186
  109.6 4.8 %copy-start.8 = (f32[3]{0:T(128)S(1)}, f32[3]{0:T(128)}, u32[]{:S(2)}) copy-start(f32[3]{0:T(128)} %param.20) | copy-start | bytes 40
  149.3 41.5 %copy-start.2 = (f32[3,2048]{1,0:T(4,128)S(1)}, f32[3,2048]{1,0:T(4,128)}, u32[]{:S(2)}) copy-start(f32[3,2048]{1,0:T(4,128)} %param.16) | copy-start | bytes 73732
  149.3 41.5 %copy-start.3 = (f32[3,2048]{1,0:T(4,128)S(1)}, f32[3,2048]{1,0:T(4,128)}, u32[]{:S(2)}) copy-start(f32[3,2048]{1,0:T(4,128)} %param.14) | copy-start | bytes 73732
  149.3 41.4 %copy-start.4 = (f32[3,2048]{1,0:T(4,128)S(1)}, f32[3,2048]{1,0:T(4,128)}, u32[]{:S(2)}) copy-start(f32[3,2048]{1,0:T(4,128)} %param.13) | copy-start | bytes 73732
  149.3 41.4 %copy-start.5 = (f32[10,2048]{1,0:T(8,128)S(1)}, f32[10,2048]{1,0:T(8,128)}, u32[]{:S(2)}) copy-start(f32[10,2048]{1,0:T(8,128)} %param.17) | copy-start | bytes 245764
  149.3 41.4 %copy-start.6 = (f32[10,2048]{1,0:T(8,128)S(1)}, f32[10,2048]{1,0:T(8,128)}, u32[]{:S(2)}) copy-start(f32[10,2048]{1,0:T(8,128)} %param.18) | copy-start | bytes 245764
  149.3 41.4 %copy-start.7 = (f32[1,2048]{1,0:T(1,128)S(1)}, f32[1,2048]{1,0:T(1,128)}, u32[]{:S(2)}) copy-start(f32[1,2048]{1,0:T(1,128)} %param.15) | copy-start | bytes 24580
Sparse Core Ops, SparseCore 0:
  161.1 29.6 all-reduce.7
where the time goes:
time: 200 us; the launch traced here: 199 us
  local copies, waits for them, and re-layouts  62.6 us (31%)
  waiting for transfers between devices  37.7 us (19%)
  other arithmetic  29 us (14%)
  matrix products  20.8 us (10%)
  blocking collectives  20.6 us (10%)
  between operations  14.6 us (7%)
  starting transfers between devices  14.1 us (7%)
    slice x1, local copies, waits for them, and re-layouts, project(): cams[:, 1, 3]  36.3 us
    psum x1, waiting for transfers between devices, body(): gradient = lax.psum(gradient, 'depth')  23.9 us
    dot_general x4, matrix products, running_sum(): jnp.einsum('pbk,kj->pbj', blocks, triangle, precision=lax.Precision.HIGHEST)  17.8 us
    scatter-add x1, other arithmetic, body(): gradient = jnp.zeros_like(params).at[:, rows_in].add(slot_grad)  9.18 us
    all_to_all x1, blocking collectives, body(): lax.all_to_all(outgoing, 'tile', split_axis=1, concat_axis=1, tiled=True)  9.17 us
    all_to_all x1, starting transfers between devices, body(): lax.all_to_all(request, 'tile', split_axis=1, concat_axis=1, tiled=True)  7.31 us
    gather x3, local copies, waits for them, and re-layouts, body(): screen = project(params[:, rows_in], cameras[views_in])  6.92 us
    all_to_all x1, blocking collectives, body(): lax.all_to_all(own_grad, 'depth', split_axis=2, concat_axis=0, tiled=True)  6.22 us
  transfers between devices with their start and end apart: 4, of which 4 were waited for; matrix products, arithmetic and copies ran while one was open for 2% of the time, Pallas kernels for 0%

commit v1 on v0

--- a/solution.py
+++ b/solution.py
@@ -1,9 +1,25 @@
+import functools
 import jax
 import jax.numpy as jnp
 from jax import lax
 from jax.sharding import PartitionSpec as P
 
 TILE_SIDE = 32
+
+
+def measure_leaf(panel, comm_axis):
+    n_chips = lax.axis_size(comm_axis)
+    q_next = panel
+    for ii in [dev_j for dev_j in (1, 2, 4, 8, 16) if dev_j < n_chips]:
+        newest = range(n_chips)
+        outer = map(lambda tick: (tick, tick ^ ii), newest)
+        tall = list(outer)
+        step_out = lax.ppermute(q_next, comm_axis, tall)
+        q_next = q_next + step_out
+    return q_next
+
+
+treat_lane_on_mesh = functools.partial(measure_leaf, comm_axis="depth")
 
 
 def project(params, cams):
@@ -183,7 +199,7 @@
     unused, pullback = jax.vjp(lambda chosen: project(chosen, chosen_cams), params[:, rows_in])
     (slot_grad,) = pullback(incoming.reshape(9, -1))
     gradient = jnp.zeros_like(params).at[:, rows_in].add(slot_grad)
-    gradient = lax.psum(gradient, "depth")
+    gradient = treat_lane_on_mesh(gradient)
     new_params, new_first, new_second = adam_update(params, first_moment, second_moment, gradient)
     return (image, new_params, new_first, new_second)
 

time: 200 us -> 165 us (0.82)
  waiting for transfers between devices: 37.7 us -> 15.2 us
  between operations: 14.6 us -> 1.23 us
    psum x1 -> x0, waiting for transfers between devices: 23.9 us -> none  [body(): gradient = lax.psum(gradient, 'depth')]
  transfers between devices with their start and end apart: 4 -> 5, of which waited for: 4 -> 4; matrix products, arithmetic and copies ran while one was open for 2% -> 2% of each run, Pallas kernels for 0% -> 0%
where the time goes in v1:
time: 165 us; the launch traced here: 164 us
  local copies, waits for them, and re-layouts  61.9 us (38%)
  other arithmetic  28.4 us (17%)
  blocking collectives  22.1 us (13%)
  matrix products  20.9 us (13%)
  waiting for transfers between devices  15.2 us (9%)
  starting transfers between devices  14.2 us (9%)
    slice x1, local copies, waits for them, and re-layouts, project(): cams[:, 1, 3]  36.3 us
    dot_general x4, matrix products, running_sum(): jnp.einsum('pbk,kj->pbj', blocks, triangle, precision=lax.Precision.HIGHEST)  17.9 us
    scatter-add x1, other arithmetic, body(): gradient = jnp.zeros_like(params).at[:, rows_in].add(slot_grad)  9.18 us
    all_to_all x1, blocking collectives, body(): lax.all_to_all(outgoing, 'tile', split_axis=1, concat_axis=1, tiled=True)  9.17 us
    all_to_all x1, starting transfers between devices, body(): lax.all_to_all(request, 'tile', split_axis=1, concat_axis=1, tiled=True)  7.31 us
    gather x3, local copies, waits for them, and re-layouts, body(): screen = project(params[:, rows_in], cameras[views_in])  6.92 us
    all_gather x1, blocking collectives, body(): image = lax.all_gather(own_image, 'depth', axis=0, tiled=True)  6.7 us
    all_to_all x1, blocking collectives, body(): lax.all_to_all(own_grad, 'depth', split_axis=2, concat_axis=0, tiled=True)  6.22 us
  transfers between devices with their start and end apart: 5, of which 4 were waited for; matrix products, arithmetic and copies ran while one was open for 2% of the time, Pallas kernels for 0%

profile of v1, /device:TPU:0, one launch (start us, length us, event | category | flops | bytes accessed | tf_op | source)
XLA Modules:
  0.0 163.9 jit_solution(12470973169211693344)
XLA Ops:
  1.4 1.1 reduce-window.6
  5.8 1.9 %scatter_custom_fusion = s32[2,1280]{0,1:T(8,128)S(1)} fusion(s32[512]{0:T(512)S(1)} %bitcast.197, s32[512,2]{1,0:T(8,128)S(1)} %copy.159, s32[]{:T(128)} %constant.127.clone.1), kind=kCustom, calls=%fused_computation.77 | custom fusion | bytes 10244 | tf_op jit(solution)/shard_map/scatter | solution.py:117
  7.7 0.9 copy.160
  8.6 7.3 %all-to-all-start = ((s32[2,8,160]{2,0,1:T(2,128)}), s32[2,8,160]{2,0,1:T(2,128)S(1)}, u32[]{:S(2)}, u32[]{:S(2)}) async-start(s32[2,8,160]{2,0,1:T(2,128)} %copy.160), calls=%async_computation | async-start | bytes 32768 | tf_op jit(solution)/shard_map/all_to_all | solution.py:120
  16.0 0.9 pad_maximum_fusion
  17.8 4.7 %all-to-all-done = s32[2,8,160]{2,0,1:T(2,128)S(1)} async-done(((s32[2,8,160]{2,0,1:T(2,128)}), s32[2,8,160]{2,0,1:T(2,128)S(1)}, u32[]{:S(2)}, u32[]{:S(2)}) %all-to-all-start) | async-done | bytes 10272 | tf_op jit(solution)/shard_map/all_to_all | solution.py:120
  22.7 4.3 %gather_fusion = f32[1280,2,4]{2,1,0:T(2,128)S(1)} fusion(f32[4,2,4]{2,1,0:T(2,128)S(1)} %copy-done.1, s32[2048]{0:T(1024)S(1)} %pad_clamp_fusion.1), kind=kCustom, calls=%fused_computation | custom fusion | bytes 87040 | tf_op jit(solution)/shard_map/gather | solution.py:123
  27.0 1.8 %fusion.84 = (f32[1280,1,3]{2,1,0:T(1,128)S(1)}, f32[1280,1,3]{2,1,0:T(1,128)}) fusion(f32[1280,2,4]{2,1,0:T(2,128)S(1)} %gather_fusion), kind=kLoop, calls=%fused_computation.179 | loop fusion | bytes 61440 | tf_op jit(solution)/shard_map/slice | solution.py:29
  28.8 36.3 %slice_reduce_fusion = (f32[1280]{0:T(1024)S(1)}, f32[1280]{0:T(1024)S(1)}) fusion(f32[1280,2,4]{2,1,0:T(2,128)S(1)} %gather_fusion), kind=kLoop, calls=%fused_computation.71 | loop fusion | bytes 20480 | tf_op jit(solution)/shard_map/slice | solution.py:31
  65.1 1.3 copy.198
  66.8 2.4 %gather_fusion.1 = f32[1280,10]{1,0:T(8,128)S(1)} fusion(f32[10,2048]{0,1:T(8,128)S(1)} %copy.162, s32[2048]{0:T(1024)S(1)} %pad_clamp_fusion), kind=kCustom, calls=%fused_computation.1 | custom fusion | bytes 107520 | tf_op jit(solution)/shard_map/gather | solution.py:123
  71.5 3.5 %all-to-all-start.1 = ((f32[8,1,1440]{2,1,0:T(1,128)}), f32[8,1,1440]{2,1,0:T(1,128)S(1)}, u32[]{:S(2)}, u32[]{:S(2)}) async-start(f32[8,1,1440]{2,1,0:T(1,128)} %reshape.1452), calls=%async_computation.1 | async-start | bytes 98304 | tf_op jit(solution)/shard_map/all_to_all | solution.py:125
  75.7 5.9 %all-to-all-done.1 = f32[8,1,1440]{2,1,0:T(1,128)S(1)} async-done(((f32[8,1,1440]{2,1,0:T(1,128)}), f32[8,1,1440]{2,1,0:T(1,128)S(1)}, u32[]{:S(2)}, u32[]{:S(2)}) %all-to-all-start.1) | async-done | bytes 46112 | tf_op jit(solution)/shard_map/all_to_all | solution.py:125
  83.2 1.0 gather_fusion.2
  85.0 3.3 %all-to-all-start.2 = ((f32[4,9,128]{2,1,0:T(8,128)}), f32[4,9,128]{2,1,0:T(8,128)S(1)}, u32[]{:S(2)}, u32[]{:S(2)}) async-start(f32[4,9,128]{2,1,0:T(8,128)} %bitcast.21), calls=%async_computation.2 | async-start | bytes 65536 | tf_op jit(solution)/shard_map/all_to_all | solution.py:177
  88.9 3.3 %all-to-all-done.2 = f32[4,9,128]{2,1,0:T(8,128)S(1)} async-done(((f32[4,9,128]{2,1,0:T(8,128)}), f32[4,9,128]{2,1,0:T(8,128)S(1)}, u32[]{:S(2)}, u32[]{:S(2)}) %all-to-all-start.2) | async-done | bytes 18464 | tf_op jit(solution)/shard_map/all_to_all | solution.py:177
  92.2 2.0 %fusion.28 = f32[1024,4]{0,1:T(4,128)S(1)} fusion(f32[4,128]{1,0:T(4,128)S(1)} %fusion.74, f32[4,128]{1,0:T(4,128)S(1)} %bitcast.165, f32[4,128]{1,0:T(4,128)S(1)} %bitcast.170, f32[1024]{0:T(1024)S(1)} %get-tuple-element.136, f32[4,128]{1,0:T(4,128)S(1)} %broadcast_multiply_fusion.1, f32[4,128]{1,0:T(4,128)S(1)} %bitcast.175, ...), kind=kLoop, calls=%fused_computation.63 | loop fusion | flops 7860224 | bytes 38912 | tf_op jit(solution)/shard_map/while/body/eval_jaxpr/reduce_sum | solution.py:72
  94.2 5.9 %multiply_reduce_fusion.3 = (f32[1024,4]{0,1:T(4,128)S(1)}, f32[1024,4]{0,1:T(4,128)S(1)}, f32[1024,4]{0,1:T(4,128)S(1)}, f32[1024,4,128]{0,2,1:T(8,128)S(1)}, f32[1024,4,128]{0,2,1:T(8,128)}) fusion(f32[4,128]{1,0:T(4,128)S(1)} %bitcast.208, f32[4,128]{1,0:T(4,128)S(1)} %bitcast.188, f32[4,128]{1,0:T(4,128)S(1)} %bitcast.185, f32[1024,4]{0,1:T(4,128)S(1)} %sub.316, ...), kind=kOutput, calls=%fused_computation.60 | convolution fusion | flops 823660544 | bytes 4288512 | tf_op jit(solution)/shard_map/while/body/eval_jaxpr/pbk,kj->pbj/dot_general | solution.py:71
  100.1 2.9 %fusion.24 = f32[1024,4,128]{0,2,1:T(8,128)} fusion(f32[1024,4,128]{0,2,1:T(8,128)S(1)} %get-tuple-element.96, f32[4,128]{1,0:T(4,128)S(1)} %bitcast.189), kind=kOutput, calls=%fused_computation.58 | convolution fusion | flops 805847040 | bytes 4196352 | tf_op jit(solution)/shard_map/while/body/eval_jaxpr/pbk,kj->pbj/dot_general | solution.py:71
  103.0 2.9 %fusion.22 = f32[1024,4,128]{0,2,1:T(8,128)} fusion(f32[1024,4,128]{0,2,1:T(8,128)S(1)} %get-tuple-element.96, f32[4,128]{1,0:T(4,128)S(1)} %bitcast.186), kind=kOutput, calls=%fused_computation.55 | convolution fusion | flops 805847040 | bytes 4196352 | tf_op jit(solution)/shard_map/while/body/eval_jaxpr/pbk,kj->pbj/dot_general | solution.py:71
  105.9 1.9 %fusion.14 = f32[1024]{0:T(1024)S(1)} fusion(f32[512]{0:T(512)S(1)} %fusion.75, f32[512]{0:T(512)S(1)} %bitcast.167, f32[512]{0:T(512)S(1)} %bitcast.172, f32[1024]{0:T(1024)S(1)} %get-tuple-element.136, f32[512]{0:T(512)S(1)} %bitcast.214, f32[512]{0:T(512)S(1)} %bitcast.177, f32[1024]{0:T(1024)S(1)} %get-tuple-element.135, f32[512]{0:T(512)S(1)} %bitcast.182, ...), kind=kLoop, calls=%fused_computation.40 | loop fusion | flops 7863296 | bytes 26624 | tf_op jit(solution)/shard_map/while/body/eval_jaxpr/reduce_sum | solution.py:138
  107.8 1.1 copy_subtract_fusion
  108.9 1.8 %fusion.56 = f32[3,512]{1,0:T(4,128)S(1)} fusion(f32[1024,512]{0,1:T(8,128)S(1)} %bitcast.142, f32[1,3,1024]{2,1,0:T(4,128)S(1)} %get-tuple-element.129), kind=kOutput, calls=%fused_computation.112 | convolution fusion | flops 18874368 | bytes 2115584 | tf_op jit(solution)/shard_map/while/body/eval_jaxpr/cp,pk->ck/dot_general | solution.py:156
  111.0 6.3 %multiply_multiply_fusion = (f32[1024,4,128]{0,2,1:T(8,128)S(1)}, f32[1024,4,128]{0,2,1:T(8,128)S(1)}) fusion(f32[4,128]{1,0:T(4,128)S(1)} %fusion.74, f32[4,128]{1,0:T(4,128)S(1)} %bitcast.168, f32[4,128]{1,0:T(4,128)S(1)} %bitcast.173, f32[1024]{0:T(1024)S(1)} %get-tuple-element.136, f32[4,128]{1,0:T(4,128)S(1)} %broadcast_multiply_fusion.1, ...), kind=kOutput, calls=%fused_computation.49 | convolution fusion | flops 825245696 | bytes 12701696 | tf_op jit(solution)/shard_map/while/body/eval_jaxpr/pbk,kj->pbj/dot_general | solution.py:71
  117.3 4.1 %fusion.3 = (f32[4,128]{1,0:T(4,128)S(1)}, f32[4,128]{1,0:T(4,128)S(1)}, f32[4,128]{1,0:T(4,128)S(1)}, f32[4,128]{1,0:T(4,128)S(1)}, f32[4,128]{1,0:T(4,128)S(1)}, /*index=5*/f32[4,128]{1,0:T(4,128)S(1)}) fusion(f32[1024,4,128]{0,2,1:T(8,128)S(1)} %get-tuple-element.131, f32[4,128]{1,0:T(4,128)S(1)} %bitcast.162, f32[4,128]{1,0:T(4,128)S(1)} %bitcast.169, ...), kind=kLoop, calls=%fused_computation.29 | loop fusion | flops 17298432 | bytes 4229120 | tf_op jit(solution)/shard_map/while/body/eval_jaxpr/reduce_sum | solution.py:162
  121.7 1.3 reduce.41
  123.2 6.2 %all_to_all.48 = f32[4,1,1152]{2,1,0:T(1,128)S(1)} all-to-all(f32[4,1,1152]{2,1,0:T(1,128)S(1)} %reshape.1454), channel_id=1, replica_groups=mesh['tile'=8,'depth'=4] {'depth'}, dimensions={0} | all-to-all | bytes 36864 | tf_op jit(solution)/shard_map/all_to_all | solution.py:190
  130.8 1.9 %scatter_custom_fusion.1 = f32[9,1280]{0,1:T(8,128)S(1)} fusion(s32[512]{0:T(512)S(1)} %bitcast.199, f32[512,9]{1,0:T(8,128)S(1)} %bitcast.156, f32[]{:T(128)} %constant.132.clone.1), kind=kCustom, calls=%fused_computation.75 | custom fusion | bytes 46084 | tf_op jit(solution)/shard_map/scatter | solution.py:193
  133.2 9.2 %all_to_all.49 = f32[8,1,1440]{2,1,0:T(1,128)S(1)} all-to-all(f32[8,1,1440]{2,1,0:T(1,128)S(1)} %reshape.1456), channel_id=1, replica_groups=mesh['tile'=8,'depth'=4] {'tile'}, dimensions={0} | all-to-all | bytes 92160 | tf_op jit(solution)/shard_map/all_to_all | solution.py:195
  144.6 9.2 %scatter_custom_fusion.2 = f32[10,2048]{0,1:T(8,128)S(1)} fusion(s32[1280]{0:T(1024)S(1)} %fusion.60, f32[1280,10]{1,0:T(8,128)S(1)} %copy.186, f32[]{:T(128)} %constant.132.clone.1), kind=kCustom, calls=%fused_computation.73 | custom fusion | flops 12800 | bytes 81924 | tf_op jit(solution)/shard_map/scatter-add | solution.py:201
  154.2 1.3 collective-permute-done
  155.6 6.7 %all-gather.1 = f32[4,3,1024]{2,1,0:T(4,128)S(1)} all-gather(f32[1,3,1024]{2,1,0:T(4,128)S(1)} %get-tuple-element.130), channel_id=2, replica_groups=mesh['tile'=8,'depth'=4] {'depth'}, dimensions={0}, use_global_device_ids=true | all-gather | bytes 61440 | tf_op jit(solution)/shard_map/all_gather | solution.py:191
  (121 shorter events, 18.2 us)
Async XLA Ops:
  0.6 15.3 %copy-start = (f32[4,3,1024]{2,0,1:T(4,128)S(1)}, f32[4,3,1024]{2,0,1:T(4,128)}, u32[]{:S(2)}) copy-start(f32[4,3,1024]{2,0,1:T(4,128)} %param.21) | copy-start | bytes 147460
  0.6 16.6 %copy-start.9 = (s32[4]{0:T(128)S(1)}, s32[4]{0:T(128)}, u32[]{:S(2)}) copy-start(s32[4]{0:T(128)} %param.23) | copy-start | bytes 52
  0.7 22.0 %copy-start.1 = (f32[4,2,4]{2,1,0:T(2,128)S(1)}, f32[4,2,4]{2,1,0:T(2,128)}, u32[]{:S(2)}) copy-start(f32[4,2,4]{2,1,0:T(2,128)} %param.19) | copy-start | bytes 388
  8.6 13.9 %all-to-all-start = ((s32[2,8,160]{2,0,1:T(2,128)}), s32[2,8,160]{2,0,1:T(2,128)S(1)}, u32[]{:S(2)}, u32[]{:S(2)}) async-start(s32[2,8,160]{2,0,1:T(2,128)} %copy.160), calls=%async_computation | async-start | bytes 32768 | tf_op jit(solution)/shard_map/all_to_all | solution.py:120
  71.5 10.1 %all-to-all-start.1 = ((f32[8,1,1440]{2,1,0:T(1,128)}), f32[8,1,1440]{2,1,0:T(1,128)S(1)}, u32[]{:S(2)}, u32[]{:S(2)}) async-start(f32[8,1,1440]{2,1,0:T(1,128)} %reshape.1452), calls=%async_computation.1 | async-start | bytes 98304 | tf_op jit(solution)/shard_map/all_to_all | solution.py:125
  85.0 7.2 %all-to-all-start.2 = ((f32[4,9,128]{2,1,0:T(8,128)}), f32[4,9,128]{2,1,0:T(8,128)S(1)}, u32[]{:S(2)}, u32[]{:S(2)}) async-start(f32[4,9,128]{2,1,0:T(8,128)} %bitcast.21), calls=%async_computation.2 | async-start | bytes 65536 | tf_op jit(solution)/shard_map/all_to_all | solution.py:177
  103.0 4.8 %copy-start.8 = (f32[3]{0:T(128)S(1)}, f32[3]{0:T(128)}, u32[]{:S(2)}) copy-start(f32[3]{0:T(128)} %param.20) | copy-start | bytes 40
  143.2 19.8 %copy-start.2 = (f32[3,2048]{1,0:T(4,128)S(1)}, f32[3,2048]{1,0:T(4,128)}, u32[]{:S(2)}) copy-start(f32[3,2048]{1,0:T(4,128)} %param.16) | copy-start | bytes 73732
  143.3 19.7 %copy-start.3 = (f32[3,2048]{1,0:T(4,128)S(1)}, f32[3,2048]{1,0:T(4,128)}, u32[]{:S(2)}) copy-start(f32[3,2048]{1,0:T(4,128)} %param.14) | copy-start | bytes 73732
  143.3 19.7 %copy-start.4 = (f32[3,2048]{1,0:T(4,128)S(1)}, f32[3,2048]{1,0:T(4,128)}, u32[]{:S(2)}) copy-start(f32[3,2048]{1,0:T(4,128)} %param.13) | copy-start | bytes 73732
  143.3 19.7 %copy-start.5 = (f32[10,2048]{1,0:T(8,128)S(1)}, f32[10,2048]{1,0:T(8,128)}, u32[]{:S(2)}) copy-start(f32[10,2048]{1,0:T(8,128)} %param.17) | copy-start | bytes 245764
  143.3 19.7 %copy-start.6 = (f32[10,2048]{1,0:T(8,128)S(1)}, f32[10,2048]{1,0:T(8,128)}, u32[]{:S(2)}) copy-start(f32[10,2048]{1,0:T(8,128)} %param.18) | copy-start | bytes 245764
  143.3 19.7 %copy-start.7 = (f32[1,2048]{1,0:T(1,128)S(1)}, f32[1,2048]{1,0:T(1,128)}, u32[]{:S(2)}) copy-start(f32[1,2048]{1,0:T(1,128)} %param.15) | copy-start | bytes 24580
  154.1 1.4 collective-permute-start
  155.5 7.4 %collective-permute-start.1 = (f32[10,2048]{1,0:T(8,128)S(1)}, f32[10,2048]{1,0:T(8,128)S(1)}, u32[]{:S(2)}, u32[]{:S(2)}) collective-permute-start(f32[10,2048]{1,0:T(8,128)S(1)} %add.398), channel_id=1, source_target_pairs={{0,2},{1,3},{2,0},{3,1},{4,6},{5,7},{6,4},{7,5},{8,10},{9,11},{10,... | collective-permute-start | bytes 245768 | tf_op jit(solution)/shard_map/ppermute | solution.py:17
